TPU v7x, 256 devices: a whole 4x4x8 slice. The times are simulated.
256 devices in a mesh: dp: 32 (over x, y, core), mp: 8 (over z).
Axes of the slice: x: 4, y: 4, z: 8, core: 2. Of those that a mesh axis runs over, the one named last changes fastest.
Arguments:
- features: bfloat16 [65536, 2, 512], P('dp'), may hold values from -27 to 27
- projection: bfloat16 [512, 256], replicated, may hold values from -1 to 1
- prototypes: float32 [3000, 256], P('mp'), may hold values from -7 to 7
Outputs:
- grad_prototypes: float32 [3000, 256], P('mp')
- grad_projection: float32 [512, 256], replicated
- loss: float32 [], replicated
All inputs are finite; a program needn't handle non-finite values.
Results may differ from a plain program's by a relative error of at most 0.0019.
The roundings to bfloat16 on the way count: a program that leaves them out, or rounds other values in their place, can miss the bound.
Values may be sent and summed in bfloat16 or wider, within the bound.
A program may use at most 128 MiB of HBM per device.

v0:
```python
import jax
import jax.numpy as jnp
from jax import lax
from jax.sharding import PartitionSpec as P

ITERS = 3
EPSILON_CODES = 0.05
SOFTMAX_TEMPER = 0.1
LOSS_FACTOR = 4096.0
TINY = 1e-06


def unit_rows(values):
    inverse = lax.rsqrt(jnp.sum(values * values, axis=-1, keepdims=True) + TINY)
    return (values * inverse, inverse)


def prototype_totals(values):
    return lax.psum(jnp.sum(values, axis=0), "dp")


def code_totals(values):
    return lax.psum(jnp.sum(values, axis=-1), "mp")


def loss_pieces(
    prototype_logits, softmax_exponent, softmax_denominator, assignments, gradient_factor
):
    swapped_targets = assignments[:, ::-1]
    grad_half = (
        (softmax_exponent / softmax_denominator[..., None] - swapped_targets) * gradient_factor
    ).astype(jnp.bfloat16)
    loss_portion = jnp.sum(
        swapped_targets
        * (prototype_logits * (1.0 / SOFTMAX_TEMPER) - jnp.log(softmax_denominator)[..., None])
    )
    return (grad_half, loss_portion)


def embed_backward(grad_unit, embed_unit, embed_inverse, own_feats):
    along_unit = jnp.sum(embed_unit * grad_unit, axis=-1, keepdims=True)
    grad_raw = ((grad_unit - embed_unit * along_unit) * embed_inverse).astype(jnp.bfloat16)
    return jnp.einsum("bve,bvp->ep", own_feats, grad_raw, preferred_element_type=jnp.float32)


def body(features, projection, prototypes):
    local_rows = features.shape[0]
    own_count = local_rows // lax.axis_size("mp")
    batch_row_count = local_rows * lax.axis_size("dp")
    gradient_factor = LOSS_FACTOR / (2.0 * batch_row_count * SOFTMAX_TEMPER)
    proto_unit, proto_inverse = unit_rows(prototypes)
    proto_half = proto_unit.astype(jnp.bfloat16)
    first_row = lax.axis_index("mp") * own_count
    own_feats = lax.dynamic_slice_in_dim(features, first_row, own_count, 0)
    raw_embed = jnp.einsum("bve,ep->bvp", own_feats, projection, preferred_element_type=jnp.float32)
    embed_unit, embed_inverse = unit_rows(raw_embed)
    embed_half = embed_unit.astype(jnp.bfloat16)
    all_embed = lax.all_gather(embed_half, "mp", axis=0, tiled=True)
    prototype_logits = jnp.einsum(
        "bvp,kp->bvk", all_embed, proto_half, preferred_element_type=jnp.float32
    )
    transport = jnp.exp(prototype_logits * (1.0 / EPSILON_CODES))
    softmax_exponent = jnp.exp(prototype_logits * (1.0 / SOFTMAX_TEMPER))
    soft_part = jnp.sum(softmax_exponent, axis=-1)
    for iteration in range(ITERS - 1):
        transport = transport / prototype_totals(transport)[None]
        transport = transport / code_totals(transport)[..., None]
    transport = transport / prototype_totals(transport)[None]
    softmax_denominator = lax.psum(soft_part, "mp")
    row_sums = code_totals(transport)
    assignments = transport / row_sums[..., None]
    grad_half, loss_portion = loss_pieces(
        prototype_logits, softmax_exponent, softmax_denominator, assignments, gradient_factor
    )
    proto_grad = jnp.einsum("bvk,bvp->kp", grad_half, all_embed, preferred_element_type=jnp.float32)
    proto_grad = lax.psum(proto_grad, "dp")
    grad_unit = lax.psum_scatter(
        jnp.einsum("bvk,kp->bvp", grad_half, proto_half, preferred_element_type=jnp.float32),
        "mp",
        scatter_dimension=0,
        tiled=True,
    )
    weight_part = embed_backward(grad_unit, embed_unit, embed_inverse, own_feats)
    weight_grad, loss_total = lax.psum((weight_part, loss_portion), ("dp", "mp"))
    along_proto = jnp.sum(proto_unit * proto_grad, axis=-1, keepdims=True)
    grad_protos = (proto_grad - proto_unit * along_proto) * proto_inverse
    loss_value = -loss_total / (2.0 * batch_row_count)
    return (grad_protos, weight_grad, loss_value)


def solution(mesh):
    return jax.shard_map(
        body,
        mesh=mesh,
        in_specs=(P("dp", None, None), P(), P("mp", None)),
        out_specs=(P("mp", None), P(), P()),
        check_vma=False,
    )
```

profile of v0, /device:TPU:2, one launch (start us, length us, event | category | flops | bytes accessed | tf_op | source)
XLA Modules:
  0.0 803.6 jit_solution(7048572155357733132)
XLA Ops:
  7.2 0.0 copy-start
  7.2 0.0 all-gather.2.cloned.1.call-start
  7.2 1.4 constant_dynamic-slice_fusion
  8.7 0.0 copy-start.3
  8.7 0.8 copy-done.3
  9.5 0.0 copy-done
  9.5 0.4 multiply_reduce_fusion.1
  9.9 0.7 multiply_convert_fusion.1
  10.6 0.0 all-gather.2.cloned.1.call-update
  10.6 0.0 reduce-scatter.2.cloned.1.call-start
  10.7 1.1 multiply_reduce_fusion.4
  11.8 49.1 %all-gather.2.cloned.1.call-done = bf16[2048,2,256]{0,2,1:T(8,128)(2,1)} async-done(((bf16[256,2,256]{0,2,1:T(8,128)(2,1)}), bf16[2048,2,256]{0,2,1:T(8,128)(2,1)}) %all-gather.2.cloned.1.call-update) | async-done | bytes 2097168 | tf_op jit(solution)/shard_map/all_gather | solution.py:58
  60.9 5.4 fusion.12
  66.3 53.0 %psum.71 = f32[2,375]{1,0:T(2,128)S(1)} all-reduce(f32[2,375]{1,0:T(2,128)S(1)} %get-tuple-element.11), channel_id=1, replica_groups=mesh['dp'=32,'mp'=8] {'dp'}, use_global_device_ids=true, to_apply=%region_5.0 | all-reduce | flops 750 | bytes 6000 | tf_op jit(solution)/shard_map/psum | solution.py:19
  119.3 3.8 exponential_reduce_fusion
  123.2 29.9 %psum.72 = f32[2048,2]{0,1:T(2,128)S(1)} all-reduce(f32[2048,2]{0,1:T(2,128)S(1)} %get-tuple-element.4), channel_id=1, replica_groups=mesh['dp'=32,'mp'=8] {'mp'}, use_global_device_ids=true, to_apply=%region_7.0 | all-reduce | flops 4096 | bytes 32768 | tf_op jit(solution)/shard_map/psum | solution.py:23
  153.0 4.4 fusion.8
  157.5 54.7 %psum.73 = f32[2,375]{1,0:T(2,128)S(1)} all-reduce(f32[2,375]{1,0:T(2,128)S(1)} %fusion.8), channel_id=1, replica_groups=mesh['dp'=32,'mp'=8] {'dp'}, use_global_device_ids=true, to_apply=%region_9.0 | all-reduce | flops 750 | bytes 6000 | tf_op jit(solution)/shard_map/psum | solution.py:19
  212.1 3.7 fusion.9
  215.9 27.0 %psum.74 = f32[2048,2]{0,1:T(2,128)S(1)} all-reduce(f32[2048,2]{0,1:T(2,128)S(1)} %fusion.9), channel_id=1, replica_groups=mesh['dp'=32,'mp'=8] {'mp'}, use_global_device_ids=true, to_apply=%region_11.0 | all-reduce | flops 4096 | bytes 32768 | tf_op jit(solution)/shard_map/psum | solution.py:23
  242.9 3.9 fusion.10
  246.8 62.7 %psum.75 = f32[2,375]{1,0:T(2,128)S(1)} all-reduce(f32[2,375]{1,0:T(2,128)S(1)} %fusion.10), channel_id=1, replica_groups=mesh['dp'=32,'mp'=8] {'dp'}, use_global_device_ids=true, to_apply=%region_13.0 | all-reduce | flops 750 | bytes 6000 | tf_op jit(solution)/shard_map/psum | solution.py:19
  309.5 4.3 fusion.11
  313.8 27.7 %all-reduce = (f32[2048,2]{0,1:T(2,128)S(1)}, f32[2048,2]{0,1:T(2,128)S(1)}) all-reduce(f32[2048,2]{0,1:T(2,128)S(1)} %fusion.11, f32[2048,2]{0,1:T(2,128)S(1)} %get-tuple-element.3), channel_id=1, replica_groups=mesh['dp'=32,'mp'=8] {'mp'}, use_global_device_ids=true, to_apply=%region_15.0 | all-reduce | flops 8192 | bytes 65536 | tf_op jit(solution)/shard_map/psum | solution.py:23
  341.5 0.0 slice-start.1
  341.5 5.1 fusion.7
  346.6 0.0 slice-done
  346.6 0.0 slice-done.1
  346.7 0.0 copy-start.2
  346.7 2.6 multiply_reduce_fusion
  349.2 1.6 copy-done.1
  350.9 0.0 copy-done.2
  350.9 3.3 fusion.28
  354.2 0.0 reduce-scatter.2.cloned.1.call-update
  354.2 0.0 all-reduce.4.cloned.1.call-start
  354.3 4.3 convolution_bitcast_fusion.1
  358.6 0.0 all-reduce.4.cloned.1.call-update
  358.7 0.0 all-reduce.6.cloned.1.call-start
  358.7 90.6 %psum.79 = f32[]{:T(128)} all-reduce(f32[]{:T(128)} %get-tuple-element.7), channel_id=1, replica_groups=mesh['dp'=32,'mp'=8] {'dp','mp'}, use_global_device_ids=true, to_apply=%region_22.0 | all-reduce | flops 1 | bytes 8 | tf_op jit(solution)/shard_map/psum | solution.py:84
  449.9 0.0 reduce-scatter.2.cloned.1.call-done
  450.0 0.0 copy-done.4
  450.0 2.5 convolution_bitcast_fusion
  452.5 0.0 all-reduce.6.cloned.1.call-update
  452.5 83.7 %all-reduce.4.cloned.1.call-done = f32[375,256]{1,0:T(8,128)} async-done(((f32[375,256]{1,0:T(8,128)}), f32[375,256]{1,0:T(8,128)}) %all-reduce.4.cloned.1.call-update) | async-done | bytes 384016 | tf_op jit(solution)/shard_map/psum | solution.py:76
  536.2 1.2 multiply_reduce_fusion.3
  537.4 1.9 subtract_multiply_fusion
  539.3 254.8 %all-reduce.6.cloned.1.call-done = f32[512,256]{1,0:T(8,128)} async-done(((f32[512,256]{1,0:T(8,128)}), f32[512,256]{1,0:T(8,128)}) %all-reduce.6.cloned.1.call-update) | async-done | bytes 524304 | tf_op jit(solution)/shard_map/psum | solution.py:84
  794.1 1.9 copy.29
  (7 shorter events, 0.0 us)
Async XLA Ops:
  7.2 2.3 copy-start
  7.2 53.7 %all-gather.2.cloned.1.call-start = ((), (), s32[]{:S(2)}) async-start(), calls=%async_computation.1 | async-start | bytes 2359296 | tf_op jit(solution)/shard_map/all_gather | solution.py:58
  8.7 0.8 copy-start.3
  10.6 439.3 %reduce-scatter.2.cloned.1.call-start = ((), (), s32[]{:S(2)}) async-start(), calls=%async_computation.3 | async-start | bytes 4718592 | tf_op jit(solution)/shard_map/reduce_scatter | solution.py:77
  309.5 37.1 %slice-start = ((s8[6160384]{0:T(1024)(128)(4,1)}), s8[1966080]{0:T(1024)(128)(4,1)S(1)}, s32[]{:S(2)}) async-start(s8[6160384]{0:T(1024)(128)(4,1)} %bitcast.19), calls=%async_computation.5 | async-start | bytes 3932160
  341.5 5.1 slice-start.1
  346.7 4.2 copy-start.2
  349.2 1.6 copy-start.1
  354.2 95.8 %copy-start.4 = (bf16[256,2,512]{2,1,0:T(2,128)(2,1)S(1)}, bf16[256,2,512]{2,1,0:T(2,128)(2,1)}, u32[]{:S(2)}) copy-start(bf16[256,2,512]{2,1,0:T(2,128)(2,1)} %copy-done.3) | copy-start | bytes 1572868
  354.2 181.9 %all-reduce.4.cloned.1.call-start = ((), (), s32[]{:S(2)}) async-start(), calls=%async_computation.2 | async-start | bytes 770048 | tf_op jit(solution)/shard_map/psum | solution.py:76
  358.7 435.4 %all-reduce.6.cloned.1.call-start = ((), (), s32[]{:S(2)}) async-start(), calls=%async_computation.4 | async-start | bytes 1048576 | tf_op jit(solution)/shard_map/psum | solution.py:84
Sparse Core Ops, SparseCore 0:
  10.7 50.1 all-gather.1
  354.4 66.9 reduce-scatter.1
  425.2 110.8 all-reduce.3
  542.1 251.9 all-reduce.5
where the time goes:
time: 804 us
  waiting for transfers between devices  388 us (48%)
  blocking collectives  345 us (43%)
  other arithmetic  32.9 us (4%)
  matrix products  16 us (2%)
  between operations  15.7 us (2%)
    psum x1, waiting for transfers between devices, body(): lax.psum((weight_part, loss_portion), ('dp', 'mp'))  255 us
    psum x3, blocking collectives, prototype_totals(): return lax.psum(jnp.sum(values, axis=0), 'dp')  170 us
    psum x1, blocking collectives, body(): lax.psum((weight_part, loss_portion), ('dp', 'mp'))  90.6 us
    psum x3, blocking collectives, code_totals(): return lax.psum(jnp.sum(values, axis=-1), 'mp')  84.6 us
    psum x1, waiting for transfers between devices, body(): proto_grad = lax.psum(proto_grad, 'dp')  83.7 us
    all_gather x1, waiting for transfers between devices, body(): all_embed = lax.all_gather(embed_half, 'mp', axis=0, tiled=True)  49.1 us
  transfers between devices with their start and end apart: 4, of which 3 were waited for; matrix products, arithmetic and copies ran while one was open for 1% of the time, Pallas kernels for 0%

commit v1 on v0

--- a/solution.py
+++ b/solution.py
@@ -73,7 +73,11 @@
         prototype_logits, softmax_exponent, softmax_denominator, assignments, gradient_factor
     )
     proto_grad = jnp.einsum("bvk,bvp->kp", grad_half, all_embed, preferred_element_type=jnp.float32)
-    proto_grad = lax.psum(proto_grad, "dp")
+    proto_grad = proto_grad
+    for hop in (1, 2, 4, 8, 16):
+        proto_grad = proto_grad + lax.ppermute(
+            proto_grad, "dp", [(dev, dev ^ hop) for dev in range(32)]
+        )
     grad_unit = lax.psum_scatter(
         jnp.einsum("bvk,kp->bvp", grad_half, proto_half, preferred_element_type=jnp.float32),
         "mp",

time: 804 us -> 745 us (0.927)
  waiting for transfers between devices: 388 us -> 328 us
  starting transfers between devices: 0.16 us -> 18.9 us
  blocking collectives: 345 us -> 330 us
    psum x1 -> x0, waiting for transfers between devices: 83.7 us -> none  [body(): proto_grad = lax.psum(proto_grad, 'dp')]
    ppermute x0 -> x5, waiting for transfers between devices: none -> 31.9 us  [body(): lax.ppermute(proto_grad, 'dp', [(dev, dev ^ hop) for dev in range(32)])]
    ppermute x0 -> x5, starting transfers between devices: none -> 18.8 us  [body(): lax.ppermute(proto_grad, 'dp', [(dev, dev ^ hop) for dev in range(32)])]
    psum x1, blocking collectives: 90.6 us -> 74.8 us  [body(): lax.psum((weight_part, loss_portion), ('dp', 'mp'))]
  transfers between devices with their start and end apart: 4 -> 8, of which waited for: 3 -> 6; matrix products, arithmetic and copies ran while one was open for 1% -> 1% of each run, Pallas kernels for 0% -> 0%
where the time goes in v1:
time: 745 us; the launch traced here: 744 us
  blocking collectives  330 us (44%)
  waiting for transfers between devices  328 us (44%)
  other arithmetic  31.2 us (4%)
  starting transfers between devices  18.9 us (3%)
  between operations  15.7 us (2%)
  matrix products  15.2 us (2%)
    psum x1, waiting for transfers between devices, body(): lax.psum((weight_part, loss_portion), ('dp', 'mp'))  247 us
    psum x3, blocking collectives, prototype_totals(): return lax.psum(jnp.sum(values, axis=0), 'dp')  170 us
    psum x3, blocking collectives, code_totals(): return lax.psum(jnp.sum(values, axis=-1), 'mp')  84.6 us
    psum x1, blocking collectives, body(): lax.psum((weight_part, loss_portion), ('dp', 'mp'))  74.8 us
    all_gather x1, waiting for transfers between devices, body(): all_embed = lax.all_gather(embed_half, 'mp', axis=0, tiled=True)  49.1 us
    ppermute x5, waiting for transfers between devices, body(): lax.ppermute(proto_grad, 'dp', [(dev, dev ^ hop) for dev in range(32)])  31.9 us
    ppermute x5, starting transfers between devices, body(): lax.ppermute(proto_grad, 'dp', [(dev, dev ^ hop) for dev in range(32)])  18.8 us
  transfers between devices with their start and end apart: 8, of which 6 were waited for; matrix products, arithmetic and copies ran while one was open for 1% of the time, Pallas kernels for 0%

profile of v1, /device:TPU:2, one launch (start us, length us, event | category | flops | bytes accessed | tf_op | source)
XLA Modules:
  0.0 744.4 jit_solution(37225807217229450)
XLA Ops:
  7.2 0.0 all-gather.2.cloned.1.call-start
  7.2 1.4 constant_dynamic-slice_fusion
  8.7 0.8 copy-done.3
  9.5 0.4 multiply_reduce_fusion.1
  9.9 0.7 multiply_convert_fusion.1
  10.6 0.0 all-gather.2.cloned.1.call-update
  10.6 0.0 reduce-scatter.2.cloned.1.call-start
  10.7 1.1 multiply_reduce_fusion.4
  11.8 49.1 %all-gather.2.cloned.1.call-done = bf16[2048,2,256]{0,2,1:T(8,128)(2,1)} async-done(((bf16[256,2,256]{0,2,1:T(8,128)(2,1)}), bf16[2048,2,256]{0,2,1:T(8,128)(2,1)}) %all-gather.2.cloned.1.call-update) | async-done | bytes 2097168 | tf_op jit(solution)/shard_map/all_gather | solution.py:58
  60.9 5.4 fusion.12
  66.3 53.0 %psum.64 = f32[2,375]{1,0:T(2,128)S(1)} all-reduce(f32[2,375]{1,0:T(2,128)S(1)} %get-tuple-element.13), channel_id=1, replica_groups=mesh['dp'=32,'mp'=8] {'dp'}, use_global_device_ids=true, to_apply=%region_5.0 | all-reduce | flops 750 | bytes 6000 | tf_op jit(solution)/shard_map/psum | solution.py:19
  119.3 3.8 exponential_reduce_fusion
  123.2 29.9 %psum.65 = f32[2048,2]{0,1:T(2,128)S(1)} all-reduce(f32[2048,2]{0,1:T(2,128)S(1)} %get-tuple-element.4), channel_id=1, replica_groups=mesh['dp'=32,'mp'=8] {'mp'}, use_global_device_ids=true, to_apply=%region_7.0 | all-reduce | flops 4096 | bytes 32768 | tf_op jit(solution)/shard_map/psum | solution.py:23
  153.0 4.4 fusion.8
  157.5 54.7 %psum.66 = f32[2,375]{1,0:T(2,128)S(1)} all-reduce(f32[2,375]{1,0:T(2,128)S(1)} %fusion.8), channel_id=1, replica_groups=mesh['dp'=32,'mp'=8] {'dp'}, use_global_device_ids=true, to_apply=%region_9.0 | all-reduce | flops 750 | bytes 6000 | tf_op jit(solution)/shard_map/psum | solution.py:19
  212.1 3.7 fusion.9
  215.9 27.0 %psum.67 = f32[2048,2]{0,1:T(2,128)S(1)} all-reduce(f32[2048,2]{0,1:T(2,128)S(1)} %fusion.9), channel_id=1, replica_groups=mesh['dp'=32,'mp'=8] {'mp'}, use_global_device_ids=true, to_apply=%region_11.0 | all-reduce | flops 4096 | bytes 32768 | tf_op jit(solution)/shard_map/psum | solution.py:23
  242.9 3.9 fusion.10
  246.8 62.7 %psum.68 = f32[2,375]{1,0:T(2,128)S(1)} all-reduce(f32[2,375]{1,0:T(2,128)S(1)} %fusion.10), channel_id=1, replica_groups=mesh['dp'=32,'mp'=8] {'dp'}, use_global_device_ids=true, to_apply=%region_13.0 | all-reduce | flops 750 | bytes 6000 | tf_op jit(solution)/shard_map/psum | solution.py:19
  309.5 4.3 fusion.11
  313.8 27.7 %all-reduce = (f32[2048,2]{0,1:T(2,128)S(1)}, f32[2048,2]{0,1:T(2,128)S(1)}) all-reduce(f32[2048,2]{0,1:T(2,128)S(1)} %fusion.11, f32[2048,2]{0,1:T(2,128)S(1)} %get-tuple-element.3), channel_id=1, replica_groups=mesh['dp'=32,'mp'=8] {'mp'}, use_global_device_ids=true, to_apply=%region_15.0 | all-reduce | flops 8192 | bytes 65536 | tf_op jit(solution)/shard_map/psum | solution.py:23
  341.5 5.1 fusion.7
  346.7 2.6 multiply_reduce_fusion
  349.2 1.6 copy-done.1
  350.9 3.3 fusion.28
  354.2 0.0 reduce-scatter.2.cloned.1.call-update
  354.3 0.0 all-reduce.3.cloned.1.call-start
  354.3 3.6 convolution_bitcast_fusion.1
  357.9 0.1 collective-permute-start
  358.0 1.7 collective-permute-done
  359.7 0.1 add.65
  359.8 0.1 collective-permute-start.1
  359.9 11.0 %collective-permute-done.1 = f32[375,256]{1,0:T(8,128)S(1)} collective-permute-done((f32[375,256]{1,0:T(8,128)S(1)}, f32[375,256]{1,0:T(8,128)S(1)}, u32[]{:S(2)}, u32[]{:S(2)}) %collective-permute-start.1) | collective-permute-done | bytes 384032 | tf_op jit(solution)/shard_map/ppermute | solution.py:78
  370.9 0.1 collective-permute-start.2
  371.0 11.6 %collective-permute-done.2 = f32[375,256]{1,0:T(8,128)S(1)} collective-permute-done((f32[375,256]{1,0:T(8,128)S(1)}, f32[375,256]{1,0:T(8,128)S(1)}, u32[]{:S(2)}, u32[]{:S(2)}) %collective-permute-start.2) | collective-permute-done | bytes 384032 | tf_op jit(solution)/shard_map/ppermute | solution.py:78
  382.6 0.1 add.67
  382.7 18.4 %collective-permute-start.3 = (f32[375,256]{1,0:T(8,128)S(1)}, f32[375,256]{1,0:T(8,128)S(1)}, u32[]{:S(2)}, u32[]{:S(2)}) collective-permute-start(f32[375,256]{1,0:T(8,128)S(1)} %add.67), channel_id=1, source_target_pairs={{0,64},{8,72},{16,80},{24,88},{32,96},{40,104},{48,112},{56,120},{... | collective-permute-start | bytes 1152008 | tf_op jit(solution)/shard_map/ppermute | solution.py:78
  401.1 7.6 %collective-permute-done.3 = f32[375,256]{1,0:T(8,128)S(1)} collective-permute-done((f32[375,256]{1,0:T(8,128)S(1)}, f32[375,256]{1,0:T(8,128)S(1)}, u32[]{:S(2)}, u32[]{:S(2)}) %collective-permute-start.3) | collective-permute-done | bytes 384032 | tf_op jit(solution)/shard_map/ppermute | solution.py:78
  408.7 0.1 add.68
  408.8 0.1 collective-permute-start.4
  408.9 74.8 %psum.71 = f32[]{:T(128)} all-reduce(f32[]{:T(128)} %get-tuple-element.9), channel_id=1, replica_groups=mesh['dp'=32,'mp'=8] {'dp','mp'}, use_global_device_ids=true, to_apply=%region_21.0 | all-reduce | flops 1 | bytes 8 | tf_op jit(solution)/shard_map/psum | solution.py:88
  484.4 0.0 reduce-scatter.2.cloned.1.call-done
  484.4 2.5 convolution_bitcast_fusion
  486.9 0.0 all-reduce.3.cloned.1.call-update
  486.9 0.2 multiply_reduce_fusion.3
  487.1 0.9 subtract_multiply_fusion
  488.1 246.8 %all-reduce.3.cloned.1.call-done = f32[512,256]{1,0:T(8,128)} async-done(((f32[512,256]{1,0:T(8,128)}), f32[512,256]{1,0:T(8,128)}) %all-reduce.3.cloned.1.call-update) | async-done | bytes 524304 | tf_op jit(solution)/shard_map/psum | solution.py:88
  734.9 1.9 copy.28
  (18 shorter events, 0.1 us)
Async XLA Ops:
  7.2 2.3 copy-start
  7.2 53.7 %all-gather.2.cloned.1.call-start = ((), (), s32[]{:S(2)}) async-start(), calls=%async_computation.1 | async-start | bytes 2359296 | tf_op jit(solution)/shard_map/all_gather | solution.py:58
  8.7 0.8 copy-start.3
  10.6 473.7 %reduce-scatter.2.cloned.1.call-start = ((), (), s32[]{:S(2)}) async-start(), calls=%async_computation.2 | async-start | bytes 4718592 | tf_op jit(solution)/shard_map/reduce_scatter | solution.py:81
  309.5 37.1 %slice-start = ((s8[6160384]{0:T(1024)(128)(4,1)}), s8[1966080]{0:T(1024)(128)(4,1)S(1)}, s32[]{:S(2)}) async-start(s8[6160384]{0:T(1024)(128)(4,1)} %bitcast.19), calls=%async_computation.4 | async-start | bytes 3932160
  341.5 5.1 slice-start.1
  346.7 4.2 copy-start.2
  349.2 1.6 copy-start.1
  354.2 130.1 %copy-start.4 = (bf16[256,2,512]{2,1,0:T(2,128)(2,1)S(1)}, bf16[256,2,512]{2,1,0:T(2,128)(2,1)}, u32[]{:S(2)}) copy-start(bf16[256,2,512]{2,1,0:T(2,128)(2,1)} %copy-done.3) | copy-start | bytes 1572868
  354.3 380.6 %all-reduce.3.cloned.1.call-start = ((), (), s32[]{:S(2)}) async-start(), calls=%async_computation.3 | async-start | bytes 1048576 | tf_op jit(solution)/shard_map/psum | solution.py:88
  357.9 1.8 collective-permute-start
  359.8 11.1 %collective-permute-start.1 = (f32[375,256]{1,0:T(8,128)S(1)}, f32[375,256]{1,0:T(8,128)S(1)}, u32[]{:S(2)}, u32[]{:S(2)}) collective-permute-start(f32[375,256]{1,0:T(8,128)S(1)} %add.65), channel_id=1, source_target_pairs={{0,16},{8,24},{16,0},{24,8},{32,48},{40,56},{48,32},{56,40},{64,80... | collective-permute-start | bytes 1152008 | tf_op jit(solution)/shard_map/ppermute | solution.py:78
  370.9 11.7 %collective-permute-start.2 = (f32[375,256]{1,0:T(8,128)S(1)}, f32[375,256]{1,0:T(8,128)S(1)}, u32[]{:S(2)}, u32[]{:S(2)}) collective-permute-start(f32[375,256]{1,0:T(8,128)S(1)} %add.66), channel_id=1, source_target_pairs={{0,32},{8,40},{16,48},{24,56},{32,0},{40,8},{48,16},{56,24},{64,96... | collective-permute-start | bytes 1152008 | tf_op jit(solution)/shard_map/ppermute | solution.py:78
  382.7 26.0 %collective-permute-start.3 = (f32[375,256]{1,0:T(8,128)S(1)}, f32[375,256]{1,0:T(8,128)S(1)}, u32[]{:S(2)}, u32[]{:S(2)}) collective-permute-start(f32[375,256]{1,0:T(8,128)S(1)} %add.67), channel_id=1, source_target_pairs={{0,64},{8,72},{16,80},{24,88},{32,96},{40,104},{48,112},{56,120},{... | collective-permute-start | bytes 1152008 | tf_op jit(solution)/shard_map/ppermute | solution.py:78
  408.8 78.1 %collective-permute-start.4 = (f32[375,256]{1,0:T(8,128)S(1)}, f32[375,256]{1,0:T(8,128)S(1)}, u32[]{:S(2)}, u32[]{:S(2)}) collective-permute-start(f32[375,256]{1,0:T(8,128)S(1)} %add.68), channel_id=1, source_target_pairs={{0,128},{8,136},{16,144},{24,152},{32,160},{40,168},{48,176},{56,1... | collective-permute-start | bytes 1152008 | tf_op jit(solution)/shard_map/ppermute | solution.py:78
Sparse Core Ops, SparseCore 0:
  10.7 50.1 all-gather.1
  354.4 66.0 reduce-scatter.1
  487.0 247.8 all-reduce.2
